TPU v7x, 32 devices: a whole 2x2x4 slice. The times are simulated.
32 devices in a mesh: section: 8 (over y, x, core), rep: 4 (over z).
Axes of the slice: x: 2, y: 2, z: 4, core: 2. Of those that a mesh axis runs over, the one named last changes fastest.
Arguments:
- features: bfloat16 [16384, 128], P('section'), may hold values from -6 to 6
- order: int32 [16384], P('section'), may hold values from 0 to 2047, as said below
- tiles: bfloat16 [8, 4, 2, 96, 128, 128], P('section', 'rep'), may hold values from -0.125 to 0.125
- tile_rows: int32 [8, 4, 2, 96], P('section', 'rep'), may hold values from 0 to 15, as said below
- tile_cols: int32 [8, 4, 2, 96], P('section', 'rep'), may hold values from 0 to 15, as said below
- live: int32 [8, 4, 2], P('section', 'rep'), may hold values from 1 to 96, as said below
- weight: bfloat16 [128, 128], replicated, may hold values from -0.5 to 0.5
- cotangent: bfloat16 [16384, 128], P('section'), may hold values from -6 to 6
Outputs:
- hidden: bfloat16 [16384, 128], P('section')
- weight_grad: float32 [128, 128], replicated
- feature_grad: bfloat16 [16384, 128], P('section')
Inputs may be any that keep to these rules, and one draw needn't show every extreme that they name: `order`: within each panel of 2048 rows, a permutation of the local row numbers. For one section, replica and round, the 96 pairs (tile_rows, tile_cols) are distinct. `tile_cols`: block column within the panel j * 4 + r for replica r and round j. Some section, replica and round has all 96 slots live.
All inputs are finite; a program needn't handle non-finite values.
Results may differ from a plain program's by a relative error of at most 0.012.
Values may be sent and summed in bfloat16 or wider, within the bound.
No kernel may reach another device: no remote copies, remote signals or barrier semaphores. Data moves between devices by JAX's collectives and lax.ppermute only.
A program may use at most 192 MiB of HBM per device.

v0:
```python
import math
import jax
import jax.numpy as jnp
from jax import lax
from jax.sharding import PartitionSpec as P


def spread(value, axis, source):
    kept = jnp.where(lax.axis_index(axis) == source, value, 0).astype(value.dtype)
    return lax.psum(kept, axis)


def shards(features, order, tiles, tile_rows, tile_cols, live, weight, cotangent):
    rep_count = lax.axis_size("rep")
    section_count = lax.axis_size("section")
    rep_index = lax.axis_index("rep")
    section_index = lax.axis_index("section")
    panel_rows, width = features.shape
    block_rows = tiles.shape[-1]
    blocks = panel_rows // block_rows
    rounds = tiles.shape[2]
    slot_count = tiles.shape[3]
    own_tiles = tiles[0, 0]
    row_table = tile_rows[0, 0]
    col_table = tile_cols[0, 0]
    live_counts = live[0, 0]
    slot_ids = jnp.arange(slot_count, dtype=jnp.int32)
    block_ids = jnp.arange(blocks, dtype=jnp.int32)
    grad_scale = 1.0 / math.sqrt(panel_rows * section_count)
    reordered = jnp.take(features, order, axis=0)

    def forward_round(round_no, running):
        root = round_no * rep_count + rep_index
        panel = spread(reordered, "section", root)
        tile_set = lax.dynamic_index_in_dim(own_tiles, round_no, 0, keepdims=False)
        row_ids = lax.dynamic_index_in_dim(row_table, round_no, 0, keepdims=False)
        col_ids = lax.dynamic_index_in_dim(col_table, round_no, 0, keepdims=False)
        count_now = lax.dynamic_index_in_dim(live_counts, round_no, 0, keepdims=False)
        picked = jnp.take(panel.reshape(blocks, block_rows, width), col_ids, axis=0)
        products = jnp.einsum("kab,kbf->kaf", tile_set, picked, preferred_element_type=jnp.float32)
        select = (
            (row_ids[None, :] == block_ids[:, None]) & (slot_ids < count_now)[None, :]
        ).astype(jnp.float32)
        return running + jnp.einsum(
            "pk,kaf->paf", select, products, precision=lax.Precision.HIGHEST
        )

    partial_sum = lax.fori_loop(
        0, rounds, forward_round, jnp.zeros((blocks, block_rows, width), jnp.float32)
    )
    partial_sum = partial_sum.reshape(panel_rows, width)
    share_rows = panel_rows // rep_count
    row_share = lax.psum_scatter(partial_sum, "rep", scatter_dimension=0, tiled=True)
    co_share = lax.dynamic_slice_in_dim(cotangent, rep_index * share_rows, share_rows, 0)
    aggregated = row_share.astype(jnp.bfloat16)
    preact = jnp.dot(aggregated, weight, preferred_element_type=jnp.float32)
    out_rows = jax.nn.silu(preact).astype(jnp.bfloat16)
    sigmoid_part = jax.nn.sigmoid(preact)
    grad_pre = (
        co_share.astype(jnp.float32) * sigmoid_part * (1.0 + preact * (1.0 - sigmoid_part))
    ).astype(jnp.bfloat16)
    grad_part = jnp.einsum("nf,ng->fg", aggregated, grad_pre, preferred_element_type=jnp.float32)
    up_rows = jnp.einsum("ng,fg->nf", grad_pre, weight, preferred_element_type=jnp.float32).astype(
        jnp.bfloat16
    )
    hidden_share, grad_part, upstream_share = (out_rows, grad_part, up_rows)
    weight_grad = lax.psum(grad_part, ("section", "rep")) * grad_scale
    hidden, upstream = (
        lax.all_gather(hidden_share, "rep", axis=0, tiled=True),
        lax.all_gather(upstream_share, "rep", axis=0, tiled=True),
    )
    up_blocks = upstream.reshape(blocks, block_rows, width)
    picked_up = jnp.take(up_blocks, row_table.reshape(-1), axis=0).reshape(
        rounds, slot_count, block_rows, width
    )
    products_back = jnp.einsum(
        "jkab,jkaf->jkbf", own_tiles, picked_up, preferred_element_type=jnp.float32
    )
    alive_mask = slot_ids[None, None, :] < live_counts[:, None, None]
    select_back = ((col_table[:, None, :] == block_ids[None, :, None]) & alive_mask).astype(
        jnp.float32
    )
    contrib = jnp.einsum(
        "jpk,jkbf->jpbf", select_back, products_back, precision=lax.Precision.HIGHEST
    )
    contrib = lax.optimization_barrier(contrib.astype(jnp.bfloat16)).astype(jnp.float32)
    contrib = contrib.reshape(rounds, panel_rows, width)
    totals = lax.psum(contrib.astype(jnp.bfloat16), "section").astype(jnp.float32)
    own_panel = lax.dynamic_index_in_dim(
        totals, section_index // rep_count, 0, keepdims=False
    ).astype(jnp.bfloat16)
    grad_rows = spread(own_panel, "rep", section_index % rep_count)
    feature_grad = jnp.zeros_like(features).at[order].set(grad_rows)
    return (hidden, weight_grad, feature_grad)


def solution(mesh):
    placed = (
        P("section", None),
        P("section"),
        P("section", "rep", None, None, None, None),
        P("section", "rep", None, None),
        P("section", "rep", None, None),
        P("section", "rep", None),
        P(),
        P("section", None),
    )
    return jax.shard_map(
        shards,
        mesh=mesh,
        in_specs=placed,
        out_specs=(P("section", None), P(), P("section", None)),
        check_vma=False,
    )
```

profile of v0, /device:TPU:0, one launch (start us, length us, event | category | flops | bytes accessed | tf_op | source)
XLA Modules:
  0.0 487.0 jit_solution(13288153377587932532)
XLA Ops:
  9.5 6.2 %gather_fusion.1 = bf16[2048,128]{1,0:T(8,128)(2,1)S(1)} fusion(bf16[2048,128]{1,0:T(8,128)(2,1)S(1)} %copy-done, s32[2048]{0:T(1024)S(1)} %get-tuple-element.296), kind=kCustom, calls=%fused_computation.1 | custom fusion | bytes 1056768 | tf_op jit(solution)/shard_map/jit(_take)/gather | solution.py:30
  16.0 147.6 %while.16 = (s32[]{:T(128)}, f32[16,128,128]{2,0,1:T(8,128)S(1)}, s32[2,96]{1,0:T(2,128)}, s32[2]{0:T(128)}, bf16[2,96,128,128]{3,2,1,0:T(8,128)(2,1)}, /*index=...) while((s32[]{:T(128)}, f32[16,128,128]{2,0,1:T(8,128)S(1)}, ...), condition=%wide.region_2.3_spmd.clone, body=%wide.region_0.0_spmd.clone.sunk | while | flops 707269568 | bytes 31465112 | solution.py:48
  20.9 57.2 %all-reduce.11.cloned.1.call-done = bf16[16,128,128]{2,1,0:T(8,128)(2,1)} async-done(((bf16[16,128,128]{2,1,0:T(8,128)(2,1)}), bf16[16,128,128]{2,1,0:T(8,128)(2,1)}) %all-reduce.11.cloned.1.call-update) | async-done | bytes 524304 | tf_op jit(solution)/shard_map/while/body/eval_jaxpr/psum | solution.py:10
  78.1 3.7 gather_fusion
  81.9 3.9 fusion.65
  85.8 5.7 %fusion.67 = f32[16,128,128]{2,0,1:T(8,128)S(1)} fusion(f32[96,128,128]{2,1,0:T(8,128)S(1)} %fusion.65, f32[16,128,128]{2,0,1:T(8,128)S(1)} %get-tuple-element.360, pred[]{:T(512)S(6)} %compare.6, s32[96]{0:T(128)S(1)} %fusion.66, pred[96]{0:T(512)(128)(4,1)S(1)} %iota_compare_fusion.5), kind=kOutput, calls=%fused_computation.14.clone.1 | convolution fusion | flops 302517248 | bytes 8389089 | tf_op jit(solution)/shard_map/while/body/eval_jaxpr/pk,kaf->paf/dot_general | solution.py:44
  96.4 53.8 %all-reduce.11.cloned.1.call-done = bf16[16,128,128]{2,1,0:T(8,128)(2,1)} async-done(((bf16[16,128,128]{2,1,0:T(8,128)(2,1)}), bf16[16,128,128]{2,1,0:T(8,128)(2,1)}) %all-reduce.11.cloned.1.call-update) | async-done | bytes 524304 | tf_op jit(solution)/shard_map/while/body/eval_jaxpr/psum | solution.py:10
  150.2 3.7 gather_fusion
  154.0 3.9 fusion.65
  157.9 5.7 %fusion.67 = f32[16,128,128]{2,0,1:T(8,128)S(1)} fusion(f32[96,128,128]{2,1,0:T(8,128)S(1)} %fusion.65, f32[16,128,128]{2,0,1:T(8,128)S(1)} %get-tuple-element.360, pred[]{:T(512)S(6)} %compare.6, s32[96]{0:T(128)S(1)} %fusion.66, pred[96]{0:T(512)(128)(4,1)S(1)} %iota_compare_fusion.5), kind=kOutput, calls=%fused_computation.14.clone.1 | convolution fusion | flops 302517248 | bytes 8389089 | tf_op jit(solution)/shard_map/while/body/eval_jaxpr/pk,kaf->paf/dot_general | solution.py:44
  167.3 25.6 %reduce-scatter.2.cloned.1.call-done = f32[512,128]{1,0:T(8,128)} async-done(((f32[2048,128]{1,0:T(8,128)}), f32[512,128]{1,0:T(8,128)}) %reduce-scatter.2.cloned.1.call-update) | async-done | bytes 262160 | tf_op jit(solution)/shard_map/reduce_scatter | solution.py:53
  194.3 16.2 %all_gather.7 = bf16[2048,128]{1,0:T(8,128)(2,1)S(1)} all-gather(bf16[512,128]{1,0:T(8,128)(2,1)S(1)} %convolution_convert_fusion), channel_id=1, replica_groups=mesh['section'=8,'rep'=4] {'rep'}, dimensions={0}, use_global_device_ids=true | all-gather | bytes 655360 | tf_op jit(solution)/shard_map/all_gather | solution.py:70
  210.5 8.0 %gather_fusion.2 = bf16[192,128,128]{2,1,0:T(8,128)(2,1)} fusion(bf16[16,128,128]{2,1,0:T(8,128)(2,1)S(1)} %bitcast.60, s32[1024]{0:T(1024)S(1)} %pad_clamp_fusion.1), kind=kCustom, calls=%fused_computation.2 | custom fusion | bytes 12583680 | tf_op jit(solution)/shard_map/jit(_take)/gather | solution.py:73
  218.5 11.6 %fusion.26 = f32[2,96,128,128]{3,2,1,0:T(8,128)} fusion(bf16[2,96,128,128]{3,2,1,0:T(8,128)(2,1)} %bitcast.64, pred[2,96]{1,0:T(4,128)(4,1)S(1)} %compare_and_fusion.2, bf16[1,1,2,96,128,128]{5,4,3,2,1,0:T(8,128)(2,1)} %bitcast.62), kind=kOutput, calls=%fused_computation.34 | convolution fusion | flops 808452096 | bytes 25166016 | tf_op jit(solution)/shard_map/jkab,jkaf->jkbf/dot_general | solution.py:76
  230.1 12.8 %copy.14 = f32[2,96,128,128]{2,1,3,0:T(8,128)} copy(f32[2,96,128,128]{3,2,1,0:T(8,128)} %fusion.26) | data formatting | bytes 25165824 | tf_op jit(solution)/shard_map/jkab,jkaf->jkbf/dot_general | solution.py:76
  242.8 7.2 %fusion.30 = bf16[2,16,128,128]{3,1,2,0:T(8,128)(2,1)S(1)} fusion(f32[2,96,128,128]{2,1,3,0:T(8,128)} %copy.14, s32[2,96]{1,0:T(2,128)S(1)} %copy-done.3, pred[2,96]{1,0:T(4,128)(4,1)S(1)} %iota_compare_fusion.3), kind=kOutput, calls=%fused_computation.38 | convolution fusion | flops 604510208 | bytes 13632448 | tf_op jit(solution)/shard_map/jpk,jkbf->jpbf/dot_general | solution.py:83
  250.1 1.3 copy.12
  252.5 53.3 %all-reduce.7.cloned.1.call-done = bf16[2,2048,128]{2,1,0:T(8,128)(2,1)} async-done(((bf16[2,2048,128]{2,1,0:T(8,128)(2,1)}), bf16[2,2048,128]{2,1,0:T(8,128)(2,1)}) %all-reduce.7.cloned.1.call-update) | async-done | bytes 1048592 | tf_op jit(solution)/shard_map/psum | solution.py:88
  305.8 1.9 fusion.34
  307.7 14.8 %all_gather.6 = bf16[2048,128]{1,0:T(8,128)(2,1)S(1)} all-gather(bf16[512,128]{1,0:T(8,128)(2,1)S(1)} %get-tuple-element.294), channel_id=1, replica_groups=mesh['section'=8,'rep'=4] {'rep'}, dimensions={0}, use_global_device_ids=true | all-gather | bytes 655360 | tf_op jit(solution)/shard_map/all_gather | solution.py:69
  322.5 106.7 %all-reduce.5.cloned.1.call-done = f32[128,128]{1,0:T(8,128)} async-done(((f32[128,128]{1,0:T(8,128)}), f32[128,128]{1,0:T(8,128)}) %all-reduce.5.cloned.1.call-update) | async-done | bytes 65552 | tf_op jit(solution)/shard_map/psum | solution.py:67
  429.3 1.5 broadcast_multiply_fusion
  430.7 41.1 %all-reduce.9.cloned.1.call-done = bf16[2048,128]{1,0:T(8,128)(2,1)} async-done(((bf16[2048,128]{1,0:T(8,128)(2,1)}), bf16[2048,128]{1,0:T(8,128)(2,1)}) %all-reduce.9.cloned.1.call-update) | async-done | bytes 524304 | tf_op jit(solution)/shard_map/psum | solution.py:10
  471.8 6.8 %scatter_custom_fusion = bf16[2048,128]{1,0:T(8,128)(2,1)} fusion(s32[2048]{0:T(1024)S(1)} %get-tuple-element.295, bf16[2048,128]{1,0:T(8,128)(2,1)} %all-reduce.9.cloned.1.call-done, bf16[]{:T(256)} %constant.190.clone.1), kind=kCustom, calls=%fused_computation.44 | custom fusion | bytes 524800 | tf_op jit(solution)/shard_map/scatter | solution.py:93
  (48 shorter events, 18.4 us)
Async XLA Ops:
  8.0 1.5 copy-start
  16.0 176.9 %copy-start.2 = (bf16[128,128]{1,0:T(8,128)(2,1)S(1)}, bf16[128,128]{1,0:T(8,128)(2,1)}, u32[]{:S(2)}) copy-start(bf16[128,128]{1,0:T(8,128)(2,1)} %param.16) | copy-start | bytes 98308
  16.0 62.1 %all-reduce.11.cloned.1.call-start = ((), (), s32[]{:S(2)}) async-start(), calls=%async_computation.5 | async-start | bytes 1048576 | tf_op jit(solution)/shard_map/while/body/eval_jaxpr/psum | solution.py:10
  91.5 58.7 %all-reduce.11.cloned.1.call-start = ((), (), s32[]{:S(2)}) async-start(), calls=%async_computation.5 | async-start | bytes 1048576 | tf_op jit(solution)/shard_map/while/body/eval_jaxpr/psum | solution.py:10
  163.6 29.2 %reduce-scatter.2.cloned.1.call-start = ((), (), s32[]{:S(2)}) async-start(), calls=%async_computation.1 | async-start | bytes 1310720 | tf_op jit(solution)/shard_map/reduce_scatter | solution.py:53
  165.0 140.7 %all-reduce.7.cloned.1.call-start = ((), (), s32[]{:S(2)}) async-start(), calls=%async_computation.3 | async-start | bytes 2097152 | tf_op jit(solution)/shard_map/psum | solution.py:88
  230.1 12.8 %copy-start.3 = (s32[2,96]{1,0:T(2,128)S(1)}, s32[2,96]{1,0:T(2,128)}, u32[]{:S(2)}) copy-start(s32[2,96]{1,0:T(2,128)} %get-tuple-element.411) | copy-start | bytes 2308
  242.8 8.7 %copy-start.1 = (f32[512,128]{1,0:T(8,128)S(1)}, f32[512,128]{1,0:T(8,128)}, u32[]{:S(2)}) copy-start(f32[512,128]{1,0:T(8,128)} %reduce-scatter.2.cloned.1.call-done) | copy-start | bytes 786436
  251.4 177.8 %all-reduce.5.cloned.1.call-start = ((), (), s32[]{:S(2)}) async-start(), calls=%async_computation.2 | async-start | bytes 131072 | tf_op jit(solution)/shard_map/psum | solution.py:67
  252.4 219.4 %all-reduce.9.cloned.1.call-start = ((), (), s32[]{:S(2)}) async-start(), calls=%async_computation.4 | async-start | bytes 1048576 | tf_op jit(solution)/shard_map/psum | solution.py:10
Sparse Core Ops, SparseCore 0:
  20.8 57.2 all-reduce.10
  96.3 53.8 all-reduce.10
Sparse Core Ops, SparseCore 1:
  166.4 26.4 reduce-scatter.1
  251.5 54.2 all-reduce.6
  312.7 116.5 all-reduce.4
  432.3 39.4 all-reduce.8
where the time goes:
time: 488 us; the launch traced here: 487 us
  waiting for transfers between devices  338 us (69%)
  local copies, waits for them, and re-layouts  49.3 us (10%)
  matrix products  40.4 us (8%)
  blocking collectives  31 us (6%)
  between operations  15.8 us (3%)
  other arithmetic  12.4 us (3%)
    psum x3, waiting for transfers between devices, spread(): return lax.psum(kept, axis)  152 us
    psum x1, waiting for transfers between devices, shards(): weight_grad = lax.psum(grad_part, ('section', 'rep')) * grad_scale  107 us
    psum x1, waiting for transfers between devices, shards(): lax.psum(contrib.astype(jnp.bfloat16), 'section').astype(jnp.float32)  53.3 us
    reduce_scatter x1, waiting for transfers between devices, shards(): lax.psum_scatter(partial_sum, 'rep', scatter_dimension=0, tiled=True)  25.6 us
    all_gather x1, blocking collectives, shards(): lax.all_gather(upstream_share, 'rep', axis=0, tiled=True)  16.2 us
    all_gather x1, blocking collectives, shards(): lax.all_gather(hidden_share, 'rep', axis=0, tiled=True)  14.8 us
    dot_general x1, local copies, waits for them, and re-layouts, shards(): jnp.einsum('jkab,jkaf->jkbf', own_tiles, picked_up, preferred_element_typ...  12.8 us
    dot_general x1, matrix products, shards(): jnp.einsum('jkab,jkaf->jkbf', own_tiles, picked_up, preferred_element_typ...  11.6 us
  transfers between devices with their start and end apart: 6, of which 6 were waited for; matrix products, arithmetic and copies ran while one was open for 3% of the time, Pallas kernels for 0%

commit v1 on v0

--- a/solution.py
+++ b/solution.py
@@ -3,6 +3,27 @@
 import jax.numpy as jnp
 from jax import lax
 from jax.sharding import PartitionSpec as P
+
+
+def gather_around(value, axis, dim):
+    peers, index, width = (lax.axis_size(axis), lax.axis_index(axis), value.shape[dim])
+    ahead = [(i, (i + 1) % peers) for i in range(peers)]
+    left = [(i, (i - 1) % peers) for i in range(peers)]
+    filled = jnp.zeros((*value.shape[:dim], peers * width, *value.shape[dim + 1 :]), value.dtype)
+    filled = lax.dynamic_update_slice_in_dim(filled, value, index * width, axis=dim)
+    from_left = from_right = value
+    half = peers // 2
+    for lap in range(1, half + 1):
+        from_left = lax.ppermute(from_left, axis, ahead)
+        filled = lax.dynamic_update_slice_in_dim(
+            filled, from_left, (index - lap) % peers * width, axis=dim
+        )
+        if lap < peers - half:
+            from_right = lax.ppermute(from_right, axis, left)
+            filled = lax.dynamic_update_slice_in_dim(
+                filled, from_right, (index + lap) % peers * width, axis=dim
+            )
+    return filled
 
 
 def spread(value, axis, source):
@@ -67,7 +88,7 @@
     weight_grad = lax.psum(grad_part, ("section", "rep")) * grad_scale
     hidden, upstream = (
         lax.all_gather(hidden_share, "rep", axis=0, tiled=True),
-        lax.all_gather(upstream_share, "rep", axis=0, tiled=True),
+        gather_around(upstream_share, "rep", 0),
     )
     up_blocks = upstream.reshape(blocks, block_rows, width)
     picked_up = jnp.take(up_blocks, row_table.reshape(-1), axis=0).reshape(

time: 488 us -> 486 us (level)
  blocking collectives: 31 us -> 14.8 us
  waiting for transfers between devices: 338 us -> 349 us
    all_gather x1 -> x0, blocking collectives: 16.2 us -> none  [shards(): lax.all_gather(upstream_share, 'rep', axis=0, tiled=True)]
    ppermute x0 -> x3, waiting for transfers between devices: none -> 10.3 us  [the longest x2 10 us: gather_around(): from_left = lax.ppermute(from_left, axis, ahead)]
  transfers between devices with their start and end apart: 6 -> 9, of which waited for: 6 -> 9; matrix products, arithmetic and copies ran while one was open for 3% -> 3% of each run, Pallas kernels for 0% -> 0%
where the time goes in v1:
time: 486 us
  waiting for transfers between devices  349 us (72%)
  local copies, waits for them, and re-layouts  49.3 us (10%)
  matrix products  40.4 us (8%)
  between operations  15.8 us (3%)
  blocking collectives  14.8 us (3%)
  other arithmetic  12.4 us (3%)
    psum x3, waiting for transfers between devices, spread(): return lax.psum(kept, axis)  152 us
    psum x1, waiting for transfers between devices, shards(): weight_grad = lax.psum(grad_part, ('section', 'rep')) * grad_scale  107 us
    psum x1, waiting for transfers between devices, shards(): lax.psum(contrib.astype(jnp.bfloat16), 'section').astype(jnp.float32)  53.3 us
    reduce_scatter x1, waiting for transfers between devices, shards(): lax.psum_scatter(partial_sum, 'rep', scatter_dimension=0, tiled=True)  26.4 us
    all_gather x1, blocking collectives, shards(): lax.all_gather(hidden_share, 'rep', axis=0, tiled=True)  14.8 us
    dot_general x1, local copies, waits for them, and re-layouts, shards(): jnp.einsum('jkab,jkaf->jkbf', own_tiles, picked_up, preferred_element_typ...  12.7 us
    dot_general x1, matrix products, shards(): jnp.einsum('jkab,jkaf->jkbf', own_tiles, picked_up, preferred_element_typ...  11.6 us
    dot_general x2, matrix products, forward_round(): jnp.einsum('pk,kaf->paf', select, products, precision=lax.Precision.HIGHEST)  11.5 us
  transfers between devices with their start and end apart: 9, of which 9 were waited for; matrix products, arithmetic and copies ran while one was open for 3% of the time, Pallas kernels for 0%

profile of v1, /device:TPU:0, one launch (start us, length us, event | category | flops | bytes accessed | tf_op | source)
XLA Modules:
  0.0 485.8 jit_solution(8076504903771594842)
XLA Ops:
  9.5 6.2 %gather_fusion.1 = bf16[2048,128]{1,0:T(8,128)(2,1)S(1)} fusion(bf16[2048,128]{1,0:T(8,128)(2,1)S(1)} %copy-done, s32[2048]{0:T(1024)S(1)} %get-tuple-element.296), kind=kCustom, calls=%fused_computation.1 | custom fusion | bytes 1056768 | tf_op jit(solution)/shard_map/jit(_take)/gather | solution.py:51
  16.0 147.5 %while.16 = (s32[]{:T(128)}, f32[16,128,128]{2,0,1:T(8,128)S(1)}, s32[2,96]{1,0:T(2,128)}, s32[2]{0:T(128)}, bf16[2,96,128,128]{3,2,1,0:T(8,128)(2,1)}, /*index=...) while((s32[]{:T(128)}, f32[16,128,128]{2,0,1:T(8,128)S(1)}, ...), condition=%wide.region_2.3_spmd.clone, body=%wide.region_0.0_spmd.clone.sunk | while | flops 707269568 | bytes 31465112 | solution.py:69
  20.9 57.2 %all-reduce.11.cloned.1.call-done = bf16[16,128,128]{2,1,0:T(8,128)(2,1)} async-done(((bf16[16,128,128]{2,1,0:T(8,128)(2,1)}), bf16[16,128,128]{2,1,0:T(8,128)(2,1)}) %all-reduce.11.cloned.1.call-update) | async-done | bytes 524304 | tf_op jit(solution)/shard_map/while/body/eval_jaxpr/psum | solution.py:31
  78.1 3.7 gather_fusion
  81.9 3.9 fusion.65
  85.8 5.7 %fusion.67 = f32[16,128,128]{2,0,1:T(8,128)S(1)} fusion(f32[96,128,128]{2,1,0:T(8,128)S(1)} %fusion.65, f32[16,128,128]{2,0,1:T(8,128)S(1)} %get-tuple-element.362, pred[]{:T(512)S(6)} %compare.9, s32[96]{0:T(128)S(1)} %fusion.66, pred[96]{0:T(512)(128)(4,1)S(1)} %iota_compare_fusion.5), kind=kOutput, calls=%fused_computation.14.clone.1 | convolution fusion | flops 302517248 | bytes 8389089 | tf_op jit(solution)/shard_map/while/body/eval_jaxpr/pk,kaf->paf/dot_general | solution.py:65
  96.4 53.8 %all-reduce.11.cloned.1.call-done = bf16[16,128,128]{2,1,0:T(8,128)(2,1)} async-done(((bf16[16,128,128]{2,1,0:T(8,128)(2,1)}), bf16[16,128,128]{2,1,0:T(8,128)(2,1)}) %all-reduce.11.cloned.1.call-update) | async-done | bytes 524304 | tf_op jit(solution)/shard_map/while/body/eval_jaxpr/psum | solution.py:31
  150.2 3.7 gather_fusion
  153.9 3.9 fusion.65
  157.8 5.7 %fusion.67 = f32[16,128,128]{2,0,1:T(8,128)S(1)} fusion(f32[96,128,128]{2,1,0:T(8,128)S(1)} %fusion.65, f32[16,128,128]{2,0,1:T(8,128)S(1)} %get-tuple-element.362, pred[]{:T(512)S(6)} %compare.9, s32[96]{0:T(128)S(1)} %fusion.66, pred[96]{0:T(512)(128)(4,1)S(1)} %iota_compare_fusion.5), kind=kOutput, calls=%fused_computation.14.clone.1 | convolution fusion | flops 302517248 | bytes 8389089 | tf_op jit(solution)/shard_map/while/body/eval_jaxpr/pk,kaf->paf/dot_general | solution.py:65
  166.4 26.4 %reduce-scatter.2.cloned.1.call-done = f32[512,128]{1,0:T(8,128)} async-done(((f32[2048,128]{1,0:T(8,128)}), f32[512,128]{1,0:T(8,128)}) %reduce-scatter.2.cloned.1.call-update) | async-done | bytes 262160 | tf_op jit(solution)/shard_map/reduce_scatter | solution.py:74
  195.2 3.8 collective-permute-start.1
  199.0 3.6 collective-permute-done
  202.9 6.4 %collective-permute-done.2 = bf16[512,128]{1,0:T(8,128)(2,1)S(1)} collective-permute-done((bf16[512,128]{1,0:T(8,128)(2,1)S(1)}, bf16[512,128]{1,0:T(8,128)(2,1)S(1)}, u32[]{:S(2)}, u32[]{:S(2)}) %collective-permute-start.2) | collective-permute-done | bytes 131104 | tf_op jit(solution)/shard_map/ppermute | solution.py:17
  209.4 8.0 %gather_fusion.2 = bf16[192,128,128]{2,1,0:T(8,128)(2,1)} fusion(bf16[16,128,128]{2,1,0:T(8,128)(2,1)S(1)} %bitcast.60, s32[1024]{0:T(1024)S(1)} %pad_clamp_fusion.1), kind=kCustom, calls=%fused_computation.2 | custom fusion | bytes 12583680 | tf_op jit(solution)/shard_map/jit(_take)/gather | solution.py:94
  217.4 11.6 %fusion.26 = f32[2,96,128,128]{3,2,1,0:T(8,128)} fusion(bf16[2,96,128,128]{3,2,1,0:T(8,128)(2,1)} %bitcast.64, pred[2,96]{1,0:T(4,128)(4,1)S(1)} %compare_and_fusion.2, bf16[1,1,2,96,128,128]{5,4,3,2,1,0:T(8,128)(2,1)} %bitcast.62), kind=kOutput, calls=%fused_computation.34 | convolution fusion | flops 808452096 | bytes 25166016 | tf_op jit(solution)/shard_map/jkab,jkaf->jkbf/dot_general | solution.py:97
  228.9 12.7 %copy.14 = f32[2,96,128,128]{2,1,3,0:T(8,128)} copy(f32[2,96,128,128]{3,2,1,0:T(8,128)} %fusion.26) | data formatting | bytes 25165824 | tf_op jit(solution)/shard_map/jkab,jkaf->jkbf/dot_general | solution.py:97
  241.6 7.2 %fusion.30 = bf16[2,16,128,128]{3,1,2,0:T(8,128)(2,1)S(1)} fusion(f32[2,96,128,128]{2,1,3,0:T(8,128)} %copy.14, s32[2,96]{1,0:T(2,128)S(1)} %copy-done.3, pred[2,96]{1,0:T(4,128)(4,1)S(1)} %iota_compare_fusion.3), kind=kOutput, calls=%fused_computation.38 | convolution fusion | flops 604510208 | bytes 13632448 | tf_op jit(solution)/shard_map/jpk,jkbf->jpbf/dot_general | solution.py:104
  251.2 53.3 %all-reduce.7.cloned.1.call-done = bf16[2,2048,128]{2,1,0:T(8,128)(2,1)} async-done(((bf16[2,2048,128]{2,1,0:T(8,128)(2,1)}), bf16[2,2048,128]{2,1,0:T(8,128)(2,1)}) %all-reduce.7.cloned.1.call-update) | async-done | bytes 1048592 | tf_op jit(solution)/shard_map/psum | solution.py:109
  304.5 1.9 fusion.34
  306.4 14.8 %all_gather.3 = bf16[2048,128]{1,0:T(8,128)(2,1)S(1)} all-gather(bf16[512,128]{1,0:T(8,128)(2,1)S(1)} %get-tuple-element.294), channel_id=1, replica_groups=mesh['section'=8,'rep'=4] {'rep'}, dimensions={0}, use_global_device_ids=true | all-gather | bytes 655360 | tf_op jit(solution)/shard_map/all_gather | solution.py:90
  321.2 106.7 %all-reduce.5.cloned.1.call-done = f32[128,128]{1,0:T(8,128)} async-done(((f32[128,128]{1,0:T(8,128)}), f32[128,128]{1,0:T(8,128)}) %all-reduce.5.cloned.1.call-update) | async-done | bytes 65552 | tf_op jit(solution)/shard_map/psum | solution.py:88
  429.5 41.1 %all-reduce.9.cloned.1.call-done = bf16[2048,128]{1,0:T(8,128)(2,1)} async-done(((bf16[2048,128]{1,0:T(8,128)(2,1)}), bf16[2048,128]{1,0:T(8,128)(2,1)}) %all-reduce.9.cloned.1.call-update) | async-done | bytes 524304 | tf_op jit(solution)/shard_map/psum | solution.py:31
  470.5 6.8 %scatter_custom_fusion = bf16[2048,128]{1,0:T(8,128)(2,1)} fusion(s32[2048]{0:T(1024)S(1)} %get-tuple-element.295, bf16[2048,128]{1,0:T(8,128)(2,1)} %all-reduce.9.cloned.1.call-done, bf16[]{:T(256)} %constant.206.clone.1), kind=kCustom, calls=%fused_computation.44 | custom fusion | bytes 524800 | tf_op jit(solution)/shard_map/scatter | solution.py:114
  (57 shorter events, 21.6 us)
Async XLA Ops:
  8.0 1.5 copy-start
  16.0 176.8 %copy-start.2 = (bf16[128,128]{1,0:T(8,128)(2,1)S(1)}, bf16[128,128]{1,0:T(8,128)(2,1)}, u32[]{:S(2)}) copy-start(bf16[128,128]{1,0:T(8,128)(2,1)} %param.16) | copy-start | bytes 98308
  16.0 62.1 %all-reduce.11.cloned.1.call-start = ((), (), s32[]{:S(2)}) async-start(), calls=%async_computation.5 | async-start | bytes 1048576 | tf_op jit(solution)/shard_map/while/body/eval_jaxpr/psum | solution.py:31
  91.5 58.7 %all-reduce.11.cloned.1.call-start = ((), (), s32[]{:S(2)}) async-start(), calls=%async_computation.5 | async-start | bytes 1048576 | tf_op jit(solution)/shard_map/while/body/eval_jaxpr/psum | solution.py:31
  163.6 29.2 %reduce-scatter.2.cloned.1.call-start = ((), (), s32[]{:S(2)}) async-start(), calls=%async_computation.1 | async-start | bytes 1310720 | tf_op jit(solution)/shard_map/reduce_scatter | solution.py:74
  164.9 139.5 %all-reduce.7.cloned.1.call-start = ((), (), s32[]{:S(2)}) async-start(), calls=%async_computation.3 | async-start | bytes 2097152 | tf_op jit(solution)/shard_map/psum | solution.py:109
  194.4 8.2 %collective-permute-start = (bf16[512,128]{1,0:T(8,128)(2,1)S(1)}, bf16[512,128]{1,0:T(8,128)(2,1)S(1)}, u32[]{:S(2)}, u32[]{:S(2)}) collective-permute-start(bf16[512,128]{1,0:T(8,128)(2,1)S(1)} %get-tuple-element.298), channel_id=1, source_target_pairs={{0,1},{1,2},{2,3},{3,0},{4,5},{5,6},{6,7},{7,4},{8,9},{9,10},{10,1... | collective-permute-start | bytes 393224 | tf_op jit(solution)/shard_map/ppermute | solution.py:17
  195.2 7.7 %collective-permute-start.1 = (bf16[512,128]{1,0:T(8,128)(2,1)S(1)}, bf16[512,128]{1,0:T(8,128)(2,1)S(1)}, u32[]{:S(2)}, u32[]{:S(2)}) collective-permute-start(bf16[512,128]{1,0:T(8,128)(2,1)S(1)} %get-tuple-element.298), channel_id=1, source_target_pairs={{0,3},{1,0},{2,1},{3,2},{4,7},{5,4},{6,5},{7,6},{8,11},{9,8},{10,9... | collective-permute-start | bytes 393224 | tf_op jit(solution)/shard_map/ppermute | solution.py:22
  202.6 6.8 %collective-permute-start.2 = (bf16[512,128]{1,0:T(8,128)(2,1)S(1)}, bf16[512,128]{1,0:T(8,128)(2,1)S(1)}, u32[]{:S(2)}, u32[]{:S(2)}) collective-permute-start(bf16[512,128]{1,0:T(8,128)(2,1)S(1)} %collective-permute-done), channel_id=1, source_target_pairs={{0,1},{1,2},{2,3},{3,0},{4,5},{5,6},{6,7},{7,4},{8,9},{9,10},{10,1... | collective-permute-start | bytes 393224 | tf_op jit(solution)/shard_map/ppermute | solution.py:17
  228.9 12.7 %copy-start.3 = (s32[2,96]{1,0:T(2,128)S(1)}, s32[2,96]{1,0:T(2,128)}, u32[]{:S(2)}) copy-start(s32[2,96]{1,0:T(2,128)} %get-tuple-element.419) | copy-start | bytes 2308
  241.6 8.7 %copy-start.1 = (f32[512,128]{1,0:T(8,128)S(1)}, f32[512,128]{1,0:T(8,128)}, u32[]{:S(2)}) copy-start(f32[512,128]{1,0:T(8,128)} %reduce-scatter.2.cloned.1.call-done) | copy-start | bytes 786436
  250.2 177.8 %all-reduce.5.cloned.1.call-start = ((), (), s32[]{:S(2)}) async-start(), calls=%async_computation.2 | async-start | bytes 131072 | tf_op jit(solution)/shard_map/psum | solution.py:88
  251.1 219.4 %all-reduce.9.cloned.1.call-start = ((), (), s32[]{:S(2)}) async-start(), calls=%async_computation.4 | async-start | bytes 1048576 | tf_op jit(solution)/shard_map/psum | solution.py:31
Sparse Core Ops, SparseCore 0:
  20.8 57.2 all-reduce.10
  96.3 53.8 all-reduce.10
Sparse Core Ops, SparseCore 1:
  166.3 26.4 reduce-scatter.1
  250.3 54.2 all-reduce.6
  311.5 116.5 all-reduce.4
  431.0 39.4 all-reduce.8
